TPU v7x, 32 devices: a whole 2x2x4 slice. The times are simulated.
32 devices in a mesh: group: 2 (over y), frame: 4 (over z), space: 2 (over x), head: 2 (over core).
Axes of the slice: x: 2, y: 2, z: 4, core: 2. Of those that a mesh axis runs over, the one named last changes fastest.
Arguments:
- queries: bfloat16 [8, 8, 48, 3072], P(('group', 'frame'), 'space', None, 'head'), parts along dimension 0, may hold values from -8 to 8
- keys: bfloat16 [8, 8, 48, 3072], P(('group', 'frame'), 'space', None, 'head'), parts along dimension 0, may hold values from -8 to 8
- values: bfloat16 [8, 8, 48, 3072], P(('group', 'frame'), 'space', None, 'head'), parts along dimension 0, may hold values from -6 to 6
- flags: int32 [4, 4], replicated, may hold values from 0 to 1, as said below
- widths: int32 [4], replicated, may hold values from 0 to 8, as said below
Outputs:
- attended: bfloat16 [8, 8, 48, 3072], P(('group', 'frame'), 'space', None, 'head'), parts along dimension 0
There are 2 independent parts, one for each index of `group`. A program takes and returns all parts, laid end to end along the dimension named above; an argument that names none is the same for every part. Nothing has to cross between parts.
Inputs may be any that keep to these rules, and one draw needn't show every extreme that they name: flags[f, g] = 1 wherever |f - g| <= 1, and flags[0, 3] = flags[3, 0] = 0. widths[0] = 8, and widths never rise with the frame distance.
All inputs are finite; a program needn't handle non-finite values.
Results may differ from a plain program's by a relative error of at most 0.006.
Values may be sent and summed in bfloat16 or wider, within the bound.
A program may use at most 128 MiB of HBM per device.

v0:
```python
import jax
import jax.numpy as jnp
from jax import lax
from jax.sharding import PartitionSpec as P

HEAD_DIM = 128
NEG_FILL = -1e30


def empty_state(leading, head_count, query_count):
    return (
        jnp.full(leading + (head_count, query_count), NEG_FILL, jnp.float32),
        jnp.zeros(leading + (head_count, query_count), jnp.float32),
        jnp.zeros(leading + (head_count, query_count, HEAD_DIM), jnp.float32),
    )


def block_update(state_old, query_heads, query_rows, reach_rows, key_block, key_rows):
    running_max, running_total, running_acc = state_old
    query_count, head_count, head_size = query_heads.shape
    key_count = key_rows.shape[0]
    score_scale = 1.0 / HEAD_DIM**0.5
    allowed = jnp.abs(query_rows[:, None] - key_rows[None, :]) <= reach_rows
    key_heads = key_block[0].reshape(key_count, head_count, head_size)
    value_heads = key_block[1].reshape(key_count, head_count, head_size)
    scores = (
        jnp.einsum("qhd,khd->hqk", query_heads, key_heads, preferred_element_type=jnp.float32)
        * score_scale
    )
    scores = jnp.where(allowed[None], scores, NEG_FILL)
    new_max = jnp.maximum(running_max, jnp.max(scores, axis=2))
    weights = jnp.where(allowed[None], jnp.exp(scores - new_max[:, :, None]), 0.0)
    rescale = jnp.exp(running_max - new_max)
    new_total = running_total * rescale + jnp.sum(weights, axis=2)
    new_acc = running_acc * rescale[:, :, None] + jnp.einsum(
        "hqk,khd->hqd",
        weights.astype(jnp.bfloat16),
        value_heads,
        preferred_element_type=jnp.float32,
    )
    return (new_max, new_total, new_acc)


def shards(queries, keys, values, flags, widths):
    frame_now = lax.axis_index("frame")
    head_query, head_key, head_value = (
        lax.all_to_all(queries, "space", split_axis=3, concat_axis=1, tiled=True),
        lax.all_to_all(keys, "space", split_axis=3, concat_axis=1, tiled=True),
        lax.all_to_all(values, "space", split_axis=3, concat_axis=1, tiled=True),
    )
    row_total = head_query.shape[1]
    columns = head_query.shape[2]
    features = head_query.shape[3]
    head_count = features // HEAD_DIM
    frame_tokens = row_total * columns
    key_rows = jnp.arange(frame_tokens, dtype=jnp.int32) // columns
    stacked = jnp.stack(
        [head_key.reshape(frame_tokens, features), head_value.reshape(frame_tokens, features)],
        axis=0,
    )[None]
    query_heads = head_query.reshape(frame_tokens, head_count, HEAD_DIM)
    flag_row = lax.dynamic_index_in_dim(flags, frame_now, 0, False)
    initial = empty_state((), head_count, frame_tokens)
    key_piece = lax.all_gather(stacked, "frame", axis=0, tiled=True)

    def advance(state_old, step_items):
        key_block, offset_now = step_items
        reach_rows = lax.dynamic_index_in_dim(widths, jnp.abs(frame_now - offset_now), 0, False)
        flag_now = lax.dynamic_index_in_dim(flag_row, offset_now, 0, False)
        state_new = lax.cond(
            flag_now > 0,
            lambda kept_state: block_update(
                kept_state, query_heads, key_rows, reach_rows, key_block, key_rows
            ),
            lambda kept_state: kept_state,
            state_old,
        )
        return (state_new, None)

    state_new, unused = lax.scan(
        advance, initial, (key_piece, jnp.arange(key_piece.shape[0], dtype=jnp.int32))
    )
    final_max, final_total, final_acc = state_new
    blended = final_acc / final_total[:, :, None]
    joined = jnp.transpose(blended, (1, 0, 2)).reshape(head_query.shape).astype(jnp.bfloat16)
    return lax.all_to_all(joined, "space", split_axis=1, concat_axis=3, tiled=True)


def solution(mesh):
    placed = (
        P(("group", "frame"), "space", None, "head"),
        P(("group", "frame"), "space", None, "head"),
        P(("group", "frame"), "space", None, "head"),
        P(),
        P(),
    )
    return jax.shard_map(
        shards,
        mesh=mesh,
        in_specs=placed,
        out_specs=P(("group", "frame"), "space", None, "head"),
        check_vma=False,
    )
```

profile of v0, /device:TPU:16, one launch (start us, length us, event | category | flops | bytes accessed | tf_op | source)
XLA Modules:
  0.0 199.9 jit_solution(7581698430664993695)
XLA Ops:
  6.5 2.6 %copy.41 = bf16[1,4,48,1536]{2,1,0,3:T(4,128)(2,1)S(1)} copy(bf16[1,4,48,1536]{3,2,1,0:T(8,128)(2,1)} %param.11) | data formatting | bytes 1179648 | tf_op args[2]
  9.1 3.4 %reshape.68 = bf16[2,2,73728]{2,1,0:T(2,128)(2,1)} reshape(bf16[1536,1,4,48]{3,2,1,0:T(4,128)(2,1)S(1)} %bitcast.61) | data formatting | bytes 1179648
  12.5 3.5 %all-to-all-start.1 = ((bf16[2,2,73728]{2,1,0:T(2,128)(2,1)}), bf16[2,2,73728]{2,1,0:T(2,128)(2,1)S(1)}, u32[]{:S(2)}, u32[]{:S(2)}) async-start(bf16[2,2,73728]{2,1,0:T(2,128)(2,1)} %reshape.68), calls=%async_computation.1 | async-start | bytes 1179648 | tf_op jit(solution)/shard_map/all_to_all | solution.py:49
  17.1 3.4 %reshape.70 = bf16[2,2,73728]{2,1,0:T(2,128)(2,1)} reshape(bf16[1536,1,4,48]{3,2,1,0:T(4,128)(2,1)S(1)} %bitcast.62) | data formatting | bytes 1179648
  20.5 4.5 %all-to-all-done.1 = bf16[2,2,73728]{2,1,0:T(2,128)(2,1)S(1)} async-done(((bf16[2,2,73728]{2,1,0:T(2,128)(2,1)}), bf16[2,2,73728]{2,1,0:T(2,128)(2,1)S(1)}, u32[]{:S(2)}, u32[]{:S(2)}) %all-to-all-start.1) | async-done | bytes 589856 | tf_op jit(solution)/shard_map/all_to_all | solution.py:49
  25.0 3.5 %all-to-all-start = ((bf16[2,2,73728]{2,1,0:T(2,128)(2,1)}), bf16[2,2,73728]{2,1,0:T(2,128)(2,1)S(1)}, u32[]{:S(2)}, u32[]{:S(2)}) async-start(bf16[2,2,73728]{2,1,0:T(2,128)(2,1)} %reshape.70), calls=%async_computation | async-start | bytes 1179648 | tf_op jit(solution)/shard_map/all_to_all | solution.py:48
  28.5 1.6 reshape.69
  31.5 5.0 %all-to-all-done = bf16[2,2,73728]{2,1,0:T(2,128)(2,1)S(1)} async-done(((bf16[2,2,73728]{2,1,0:T(2,128)(2,1)}), bf16[2,2,73728]{2,1,0:T(2,128)(2,1)S(1)}, u32[]{:S(2)}, u32[]{:S(2)}) %all-to-all-start) | async-done | bytes 589856 | tf_op jit(solution)/shard_map/all_to_all | solution.py:48
  36.6 1.6 reshape.71
  41.8 3.4 %reshape.72 = bf16[2,2,73728]{2,1,0:T(2,128)(2,1)} reshape(bf16[1536,1,4,48]{3,2,1,0:T(4,128)(2,1)S(1)} %bitcast.63) | data formatting | bytes 1179648
  45.2 3.7 %all-to-all-start.2 = ((bf16[2,2,73728]{2,1,0:T(2,128)(2,1)}), bf16[2,2,73728]{2,1,0:T(2,128)(2,1)S(1)}, u32[]{:S(2)}, u32[]{:S(2)}) async-start(bf16[2,2,73728]{2,1,0:T(2,128)(2,1)} %reshape.72), calls=%async_computation.2 | async-start | bytes 1179648 | tf_op jit(solution)/shard_map/all_to_all | solution.py:47
  48.9 7.0 %all-to-all-done.2 = bf16[2,2,73728]{2,1,0:T(2,128)(2,1)S(1)} async-done(((bf16[2,2,73728]{2,1,0:T(2,128)(2,1)}), bf16[2,2,73728]{2,1,0:T(2,128)(2,1)S(1)}, u32[]{:S(2)}, u32[]{:S(2)}) %all-to-all-start.2) | async-done | bytes 589856 | tf_op jit(solution)/shard_map/all_to_all | solution.py:47
  59.0 69.8 %all-gather.3.cloned.1.call-done = bf16[8,384,768]{2,1,0:T(8,128)(2,1)} async-done(((bf16[2,384,768]{2,1,0:T(8,128)(2,1)}), bf16[8,384,768]{2,1,0:T(8,128)(2,1)}) %all-gather.3.cloned.1.call-update) | async-done | bytes 4718608 | tf_op jit(solution)/shard_map/all_gather | solution.py:64
  128.8 6.6 %copy.46 = bf16[4,2,384,768]{2,3,1,0:T(8,128)(2,1)} copy(bf16[4,2,384,768]{3,2,1,0:T(8,128)(2,1)} %bitcast.64) | data formatting | bytes 9437184
  135.6 43.9 %while.15 = (s32[]{:T(128)}, f32[6,384]{1,0:T(8,128)S(1)}, f32[6,384]{1,0:T(8,128)S(1)}, f32[6,384,128]{2,1,0:T(8,128)S(1)}, s32[4]{0:T(128)S(1)}, /*index=5*/s3...) while((s32[]{:T(128)}, f32[6,384]{1,0:T(8,128)S(1)}, ...), condition=%wide.region_5.6_spmd.clone, body=%wide.region_0.5_spmd.clone.sunk | while | flops 465526272 | bytes 17858036 | solution.py:80
  139.5 7.1 %conditional.3 = ((f32[6,384]{1,0:T(8,128)S(1)}, f32[6,384]{1,0:T(8,128)S(1)}, f32[6,384,128]{2,1,0:T(8,128)S(1)})) conditional(s32[]{:T(128)} %bitcast.55, (f32[6,384]{1,0:T(8,128)S(1)}, f32[6,384]{1,0:T(8,128)S(1)}, f32[6,384,128]{2,1,0:T(8,128)S(1)}) %tuple.48, (s32[384]{0:T(512)S(1)}, s32[]{:T(128)}, s32[]{:T(128)}, s32[4]{0:T(128)S(1)}, ...), branch_computations={%region_1.1_spmd, %region_2.4_spmd.clone} | conditional | flops 465525888 | bytes 17853058 | solution.py:70
  144.9 1.7 fusion.12
  150.4 7.1 %conditional.3 = ((f32[6,384]{1,0:T(8,128)S(1)}, f32[6,384]{1,0:T(8,128)S(1)}, f32[6,384,128]{2,1,0:T(8,128)S(1)})) conditional(s32[]{:T(128)} %bitcast.55, (f32[6,384]{1,0:T(8,128)S(1)}, f32[6,384]{1,0:T(8,128)S(1)}, f32[6,384,128]{2,1,0:T(8,128)S(1)}) %tuple.48, (s32[384]{0:T(512)S(1)}, s32[]{:T(128)}, s32[]{:T(128)}, s32[4]{0:T(128)S(1)}, ...), branch_computations={%region_1.1_spmd, %region_2.4_spmd.clone} | conditional | flops 465525888 | bytes 17853058 | solution.py:70
  155.8 1.7 fusion.12
  161.4 7.1 %conditional.3 = ((f32[6,384]{1,0:T(8,128)S(1)}, f32[6,384]{1,0:T(8,128)S(1)}, f32[6,384,128]{2,1,0:T(8,128)S(1)})) conditional(s32[]{:T(128)} %bitcast.55, (f32[6,384]{1,0:T(8,128)S(1)}, f32[6,384]{1,0:T(8,128)S(1)}, f32[6,384,128]{2,1,0:T(8,128)S(1)}) %tuple.48, (s32[384]{0:T(512)S(1)}, s32[]{:T(128)}, s32[]{:T(128)}, s32[4]{0:T(128)S(1)}, ...), branch_computations={%region_1.1_spmd, %region_2.4_spmd.clone} | conditional | flops 465525888 | bytes 17853058 | solution.py:70
  166.8 1.7 fusion.12
  172.4 7.1 %conditional.3 = ((f32[6,384]{1,0:T(8,128)S(1)}, f32[6,384]{1,0:T(8,128)S(1)}, f32[6,384,128]{2,1,0:T(8,128)S(1)})) conditional(s32[]{:T(128)} %bitcast.55, (f32[6,384]{1,0:T(8,128)S(1)}, f32[6,384]{1,0:T(8,128)S(1)}, f32[6,384,128]{2,1,0:T(8,128)S(1)}) %tuple.48, (s32[384]{0:T(512)S(1)}, s32[]{:T(128)}, s32[]{:T(128)}, s32[4]{0:T(128)S(1)}, ...), branch_computations={%region_1.1_spmd, %region_2.4_spmd.clone} | conditional | flops 465525888 | bytes 17853058 | solution.py:70
  177.8 1.7 fusion.12
  181.0 11.2 %all_to_all.63 = bf16[1,8,48,768]{3,2,0,1:T(8,128)(2,1)S(1)} all-to-all(bf16[1,8,48,768]{3,2,0,1:T(8,128)(2,1)S(1)} %bitcast.70), channel_id=1, replica_groups=mesh['group'=2,'frame'=4,'space'=2,'head'=2] {'space'}, dimensions={1} | all-to-all | bytes 1179648 | tf_op jit(solution)/shard_map/all_to_all | solution.py:86
  (86 shorter events, 35.3 us)
Async XLA Ops:
  6.5 42.4 %copy-start = (s32[4,4]{1,0:T(4,128)S(1)}, s32[4,4]{1,0:T(4,128)}, u32[]{:S(2)}) copy-start(s32[4,4]{1,0:T(4,128)} %param.12) | copy-start | bytes 196
  6.5 9.5 %copy-start.1 = (bf16[1,4,48,1536]{3,2,1,0:T(8,128)(2,1)S(1)}, bf16[1,4,48,1536]{3,2,1,0:T(8,128)(2,1)}, u32[]{:S(2)}) copy-start(bf16[1,4,48,1536]{3,2,1,0:T(8,128)(2,1)} %param.10) | copy-start | bytes 1769476
  12.5 12.4 %all-to-all-start.1 = ((bf16[2,2,73728]{2,1,0:T(2,128)(2,1)}), bf16[2,2,73728]{2,1,0:T(2,128)(2,1)S(1)}, u32[]{:S(2)}, u32[]{:S(2)}) async-start(bf16[2,2,73728]{2,1,0:T(2,128)(2,1)} %reshape.68), calls=%async_computation.1 | async-start | bytes 1179648 | tf_op jit(solution)/shard_map/all_to_all | solution.py:49
  25.0 11.6 %all-to-all-start = ((bf16[2,2,73728]{2,1,0:T(2,128)(2,1)}), bf16[2,2,73728]{2,1,0:T(2,128)(2,1)S(1)}, u32[]{:S(2)}, u32[]{:S(2)}) async-start(bf16[2,2,73728]{2,1,0:T(2,128)(2,1)} %reshape.70), calls=%async_computation | async-start | bytes 1179648 | tf_op jit(solution)/shard_map/all_to_all | solution.py:48
  28.5 100.4 %all-gather.3.cloned.1.call-start = ((), (), s32[]{:S(2)}) async-start(), calls=%async_computation.4 | async-start | bytes 5898240 | tf_op jit(solution)/shard_map/all_gather | solution.py:64
  38.1 2.6 %copy-start.2 = (bf16[1,4,48,1536]{3,2,1,0:T(8,128)(2,1)S(1)}, bf16[1,4,48,1536]{3,2,1,0:T(8,128)(2,1)}, u32[]{:S(2)}) copy-start(bf16[1,4,48,1536]{3,2,1,0:T(8,128)(2,1)} %param.9) | copy-start | bytes 1769476
  45.2 10.7 %all-to-all-start.2 = ((bf16[2,2,73728]{2,1,0:T(2,128)(2,1)}), bf16[2,2,73728]{2,1,0:T(2,128)(2,1)S(1)}, u32[]{:S(2)}, u32[]{:S(2)}) async-start(bf16[2,2,73728]{2,1,0:T(2,128)(2,1)} %reshape.72), calls=%async_computation.2 | async-start | bytes 1179648 | tf_op jit(solution)/shard_map/all_to_all | solution.py:47
  128.8 6.7 %copy-start.3 = (s32[4]{0:T(128)S(1)}, s32[4]{0:T(128)}, u32[]{:S(2)}) copy-start(s32[4]{0:T(128)} %param.13) | copy-start | bytes 52
Sparse Core Ops, SparseCore 0:
  40.8 87.9 all-gather.2
where the time goes:
time: 201 us; the launch traced here: 200 us
  waiting for transfers between devices  86.3 us (43%)
  local copies, waits for them, and re-layouts  45.4 us (23%)
  between operations  13.6 us (7%)
  loops' own time  13.4 us (7%)
  blocking collectives  11.2 us (6%)
  starting transfers between devices  10.8 us (5%)
  matrix products  10.3 us (5%)
  other arithmetic  8.87 us (4%)
    all_gather x1, waiting for transfers between devices, shards(): key_piece = lax.all_gather(stacked, 'frame', axis=0, tiled=True)  69.8 us
    unnamed x19, local copies, waits for them, and re-layouts  26.3 us
    all_to_all x1, blocking collectives, shards(): lax.all_to_all(joined, 'space', split_axis=1, concat_axis=3, tiled=True)  11.2 us
    another operation x1, loops' own time, shards(): lax.scan(advance, initial, (key_piece, jnp.arange(key_piece.shape[0], dty...  10.5 us
    all_to_all x1, waiting for transfers between devices, shards(): lax.all_to_all(queries, 'space', split_axis=3, concat_axis=1, tiled=True)  6.99 us
    dot_general x4, matrix products, block_update(): jnp.einsum('hqk,khd->hqd', weights.astype(jnp.bfloat16), value_heads, pre...  6.73 us
    slice x4, local copies, waits for them, and re-layouts, block_update(): value_heads = key_block[1].reshape(key_count, head_count, head_size)  5.48 us
    all_to_all x1, waiting for transfers between devices, shards(): lax.all_to_all(keys, 'space', split_axis=3, concat_axis=1, tiled=True)  5.03 us
  transfers between devices with their start and end apart: 4, of which 4 were waited for; matrix products, arithmetic and copies ran while one was open for 7% of the time, Pallas kernels for 0%

commit v1 on v0

--- a/solution.py
+++ b/solution.py
@@ -5,6 +5,24 @@
 
 HEAD_DIM = 128
 NEG_FILL = -1e30
+
+
+def collect(array, axis, dim):
+    ways, here, step = (lax.axis_size(axis), lax.axis_index(axis), array.shape[dim])
+    lengths = [n * ways if d == dim else n for d, n in enumerate(array.shape)]
+    full = lax.dynamic_update_slice_in_dim(
+        jnp.zeros(lengths, array.dtype), array, here * step, axis=dim
+    )
+    going_up = going_down = array
+    for far in range(1, ways // 2 + 1):
+        going_up = lax.ppermute(going_up, axis, [(d, (d + 1) % ways) for d in range(ways)])
+        full = lax.dynamic_update_slice_in_dim(full, going_up, (here - far) % ways * step, axis=dim)
+        if 2 * far < ways:
+            going_down = lax.ppermute(going_down, axis, [(d, (d - 1) % ways) for d in range(ways)])
+            full = lax.dynamic_update_slice_in_dim(
+                full, going_down, (here + far) % ways * step, axis=dim
+            )
+    return full
 
 
 def empty_state(leading, head_count, query_count):
@@ -61,7 +79,7 @@
     query_heads = head_query.reshape(frame_tokens, head_count, HEAD_DIM)
     flag_row = lax.dynamic_index_in_dim(flags, frame_now, 0, False)
     initial = empty_state((), head_count, frame_tokens)
-    key_piece = lax.all_gather(stacked, "frame", axis=0, tiled=True)
+    key_piece = collect(stacked, "frame", 0)
 
     def advance(state_old, step_items):
         key_block, offset_now = step_items

time: 201 us -> 174 us (0.87)
  waiting for transfers between devices: 86.3 us -> 63.9 us
  between operations: 13.6 us -> 0.33 us
  local copies, waits for them, and re-layouts: 45.4 us -> 52.7 us
  starting transfers between devices: 10.8 us -> 14.4 us
    all_gather x1 -> x0, waiting for transfers between devices: 69.8 us -> none  [shards(): key_piece = lax.all_gather(stacked, 'frame', axis=0, tiled=True)]
    ppermute x0 -> x3, waiting for transfers between devices: none -> 49.5 us  [the longest x2 49.5 us: collect(): lax.ppermute(going_up, axis, [(d, (d + 1) % ways) for d in range(ways)])]
    unnamed x19 -> x18, local copies, waits for them, and re-layouts: 26.3 us -> 19.6 us
    ppermute x0 -> x3, local copies, waits for them, and re-layouts: none -> 5.1 us  [the longest x2 3.4 us: collect(): lax.ppermute(going_up, axis, [(d, (d + 1) % ways) for d in range(ways)])]
    dynamic_update_slice x0 -> x4, local copies, waits for them, and re-layouts: none -> 4.61 us  [the longest x2 2.31 us: collect(): lax.dynamic_update_slice_in_dim(full, going_up, (here - far) % ways * ste...]
    broadcast_in_dim x0 -> x2, local copies, waits for them, and re-layouts: none -> 4.23 us  [the longest x1 2.53 us: collect(): jnp.zeros(lengths, array.dtype)]
    ppermute x0 -> x3, starting transfers between devices: none -> 3.71 us  [the longest x2 3.26 us: collect(): lax.ppermute(going_up, axis, [(d, (d + 1) % ways) for d in range(ways)])]
    all_to_all x1, waiting for transfers between devices: 6.99 us -> 4.94 us  [shards(): lax.all_to_all(queries, 'space', split_axis=3, concat_axis=1, tiled=True)]
  transfers between devices with their start and end apart: 4 -> 6, of which waited for: 4 -> 4; matrix products, arithmetic and copies ran while one was open for 7% -> 15% of each run, Pallas kernels for 0% -> 0%
where the time goes in v1:
time: 174 us; the launch traced here: 173 us
  waiting for transfers between devices  63.9 us (37%)
  local copies, waits for them, and re-layouts  52.7 us (30%)
  starting transfers between devices  14.4 us (8%)
  loops' own time  13.4 us (8%)
  matrix products  10.2 us (6%)
  blocking collectives  9.35 us (5%)
  other arithmetic  8.92 us (5%)
    ppermute x2, waiting for transfers between devices, collect(): lax.ppermute(going_up, axis, [(d, (d + 1) % ways) for d in range(ways)])  49.5 us
    unnamed x18, local copies, waits for them, and re-layouts  19.6 us
    another operation x1, loops' own time, shards(): lax.scan(advance, initial, (key_piece, jnp.arange(key_piece.shape[0], dty...  10.5 us
    all_to_all x1, blocking collectives, shards(): lax.all_to_all(joined, 'space', split_axis=1, concat_axis=3, tiled=True)  9.35 us
    dot_general x4, matrix products, block_update(): jnp.einsum('hqk,khd->hqd', weights.astype(jnp.bfloat16), value_heads, pre...  6.68 us
    slice x4, local copies, waits for them, and re-layouts, block_update(): value_heads = key_block[1].reshape(key_count, head_count, head_size)  5.48 us
    all_to_all x1, waiting for transfers between devices, shards(): lax.all_to_all(keys, 'space', split_axis=3, concat_axis=1, tiled=True)  5.07 us
    all_to_all x1, waiting for transfers between devices, shards(): lax.all_to_all(queries, 'space', split_axis=3, concat_axis=1, tiled=True)  4.94 us
  transfers between devices with their start and end apart: 6, of which 4 were waited for; matrix products, arithmetic and copies ran while one was open for 15% of the time, Pallas kernels for 0%

profile of v1, /device:TPU:16, one launch (start us, length us, event | category | flops | bytes accessed | tf_op | source)
XLA Modules:
  0.0 173.3 jit_solution(11444955918683720375)
XLA Ops:
  0.0 2.6 %copy.47 = bf16[1,4,48,1536]{2,1,0,3:T(4,128)(2,1)S(1)} copy(bf16[1,4,48,1536]{3,2,1,0:T(8,128)(2,1)} %param.11) | data formatting | bytes 1179648 | tf_op args[2]
  2.6 3.4 %reshape.67 = bf16[2,2,73728]{2,1,0:T(2,128)(2,1)} reshape(bf16[1536,1,4,48]{3,2,1,0:T(4,128)(2,1)S(1)} %bitcast.62) | data formatting | bytes 1179648
  6.0 3.5 %all-to-all-start.1 = ((bf16[2,2,73728]{2,1,0:T(2,128)(2,1)}), bf16[2,2,73728]{2,1,0:T(2,128)(2,1)S(1)}, u32[]{:S(2)}, u32[]{:S(2)}) async-start(bf16[2,2,73728]{2,1,0:T(2,128)(2,1)} %reshape.67), calls=%async_computation.1 | async-start | bytes 1179648 | tf_op jit(solution)/shard_map/all_to_all | solution.py:67
  10.6 3.4 %reshape.69 = bf16[2,2,73728]{2,1,0:T(2,128)(2,1)} reshape(bf16[1536,1,4,48]{3,2,1,0:T(4,128)(2,1)S(1)} %bitcast.63) | data formatting | bytes 1179648
  14.0 4.5 %all-to-all-done.1 = bf16[2,2,73728]{2,1,0:T(2,128)(2,1)S(1)} async-done(((bf16[2,2,73728]{2,1,0:T(2,128)(2,1)}), bf16[2,2,73728]{2,1,0:T(2,128)(2,1)S(1)}, u32[]{:S(2)}, u32[]{:S(2)}) %all-to-all-start.1) | async-done | bytes 589856 | tf_op jit(solution)/shard_map/all_to_all | solution.py:67
  18.4 3.5 %all-to-all-start = ((bf16[2,2,73728]{2,1,0:T(2,128)(2,1)}), bf16[2,2,73728]{2,1,0:T(2,128)(2,1)S(1)}, u32[]{:S(2)}, u32[]{:S(2)}) async-start(bf16[2,2,73728]{2,1,0:T(2,128)(2,1)} %reshape.69), calls=%async_computation | async-start | bytes 1179648 | tf_op jit(solution)/shard_map/all_to_all | solution.py:66
  24.9 5.1 %all-to-all-done = bf16[2,2,73728]{2,1,0:T(2,128)(2,1)S(1)} async-done(((bf16[2,2,73728]{2,1,0:T(2,128)(2,1)}), bf16[2,2,73728]{2,1,0:T(2,128)(2,1)S(1)}, u32[]{:S(2)}, u32[]{:S(2)}) %all-to-all-start) | async-done | bytes 589856 | tf_op jit(solution)/shard_map/all_to_all | solution.py:66
  36.2 49.5 %collective-permute-done = bf16[1,2,384,768]{3,2,1,0:T(8,128)(2,1)} collective-permute-done((bf16[1,2,384,768]{3,2,1,0:T(8,128)(2,1)}, bf16[1,2,384,768]{3,2,1,0:T(8,128)(2,1)}, u32[]{:S(2)}, u32[]{:S(2)}) %collective-permute-start) | collective-permute-done | bytes 1179680 | tf_op jit(solution)/shard_map/ppermute | solution.py:18
  85.6 1.7 collective-permute-start.2
  88.4 3.4 %reshape.71 = bf16[2,2,73728]{2,1,0:T(2,128)(2,1)} reshape(bf16[1536,1,4,48]{3,2,1,0:T(4,128)(2,1)S(1)} %bitcast.64) | data formatting | bytes 1179648
  91.8 3.7 %all-to-all-start.2 = ((bf16[2,2,73728]{2,1,0:T(2,128)(2,1)}), bf16[2,2,73728]{2,1,0:T(2,128)(2,1)S(1)}, u32[]{:S(2)}, u32[]{:S(2)}) async-start(bf16[2,2,73728]{2,1,0:T(2,128)(2,1)} %reshape.71), calls=%async_computation.2 | async-start | bytes 1179648 | tf_op jit(solution)/shard_map/all_to_all | solution.py:65
  95.6 1.7 copy.50
  97.3 4.9 %all-to-all-done.2 = bf16[2,2,73728]{2,1,0:T(2,128)(2,1)S(1)} async-done(((bf16[2,2,73728]{2,1,0:T(2,128)(2,1)}), bf16[2,2,73728]{2,1,0:T(2,128)(2,1)S(1)}, u32[]{:S(2)}, u32[]{:S(2)}) %all-to-all-start.2) | async-done | bytes 589856 | tf_op jit(solution)/shard_map/all_to_all | solution.py:65
  105.3 2.5 %broadcast_in_dim.50 = bf16[4,2,384,768]{2,3,1,0:T(8,128)(2,1)} broadcast(bf16[]{:T(256)} %constant.83.clone.1), dimensions={} | broadcast | bytes 4718594 | tf_op jit(solution)/shard_map/broadcast_in_dim | solution.py:14
  109.0 1.7 copy.51
  110.7 1.7 copy.52
  114.7 1.7 copy.53
  117.7 43.9 %while.15 = (s32[]{:T(128)}, f32[6,384]{1,0:T(8,128)S(1)}, f32[6,384]{1,0:T(8,128)S(1)}, f32[6,384,128]{2,1,0:T(8,128)S(1)}, s32[4]{0:T(128)S(1)}, /*index=5*/s3...) while((s32[]{:T(128)}, f32[6,384]{1,0:T(8,128)S(1)}, ...), condition=%wide.region_5.6_spmd.clone, body=%wide.region_0.5_spmd.clone.sunk | while | flops 465526272 | bytes 17858036 | solution.py:98
  121.6 7.1 %conditional.3 = ((f32[6,384]{1,0:T(8,128)S(1)}, f32[6,384]{1,0:T(8,128)S(1)}, f32[6,384,128]{2,1,0:T(8,128)S(1)})) conditional(s32[]{:T(128)} %bitcast.56, (f32[6,384]{1,0:T(8,128)S(1)}, f32[6,384]{1,0:T(8,128)S(1)}, f32[6,384,128]{2,1,0:T(8,128)S(1)}) %tuple.48, (s32[384]{0:T(512)S(1)}, s32[]{:T(128)}, s32[]{:T(128)}, s32[4]{0:T(128)S(1)}, ...), branch_computations={%region_1.1_spmd, %region_2.4_spmd.clone} | conditional | flops 465525888 | bytes 17853058 | solution.py:88
  132.5 7.1 %conditional.3 = ((f32[6,384]{1,0:T(8,128)S(1)}, f32[6,384]{1,0:T(8,128)S(1)}, f32[6,384,128]{2,1,0:T(8,128)S(1)})) conditional(s32[]{:T(128)} %bitcast.56, (f32[6,384]{1,0:T(8,128)S(1)}, f32[6,384]{1,0:T(8,128)S(1)}, f32[6,384,128]{2,1,0:T(8,128)S(1)}) %tuple.48, (s32[384]{0:T(512)S(1)}, s32[]{:T(128)}, s32[]{:T(128)}, s32[4]{0:T(128)S(1)}, ...), branch_computations={%region_1.1_spmd, %region_2.4_spmd.clone} | conditional | flops 465525888 | bytes 17853058 | solution.py:88
  137.9 1.7 fusion.12
  143.5 7.1 %conditional.3 = ((f32[6,384]{1,0:T(8,128)S(1)}, f32[6,384]{1,0:T(8,128)S(1)}, f32[6,384,128]{2,1,0:T(8,128)S(1)})) conditional(s32[]{:T(128)} %bitcast.56, (f32[6,384]{1,0:T(8,128)S(1)}, f32[6,384]{1,0:T(8,128)S(1)}, f32[6,384,128]{2,1,0:T(8,128)S(1)}) %tuple.48, (s32[384]{0:T(512)S(1)}, s32[]{:T(128)}, s32[]{:T(128)}, s32[4]{0:T(128)S(1)}, ...), branch_computations={%region_1.1_spmd, %region_2.4_spmd.clone} | conditional | flops 465525888 | bytes 17853058 | solution.py:88
  154.5 7.1 %conditional.3 = ((f32[6,384]{1,0:T(8,128)S(1)}, f32[6,384]{1,0:T(8,128)S(1)}, f32[6,384,128]{2,1,0:T(8,128)S(1)})) conditional(s32[]{:T(128)} %bitcast.56, (f32[6,384]{1,0:T(8,128)S(1)}, f32[6,384]{1,0:T(8,128)S(1)}, f32[6,384,128]{2,1,0:T(8,128)S(1)}) %tuple.48, (s32[384]{0:T(512)S(1)}, s32[]{:T(128)}, s32[]{:T(128)}, s32[4]{0:T(128)S(1)}, ...), branch_computations={%region_1.1_spmd, %region_2.4_spmd.clone} | conditional | flops 465525888 | bytes 17853058 | solution.py:88
  163.0 9.3 %all_to_all.63 = bf16[1,8,48,768]{3,2,0,1:T(8,128)(2,1)S(1)} all-to-all(bf16[1,8,48,768]{3,2,0,1:T(8,128)(2,1)S(1)} %bitcast.70), channel_id=1, replica_groups=mesh['group'=2,'frame'=4,'space'=2,'head'=2] {'space'}, dimensions={1} | all-to-all | bytes 1179648 | tf_op jit(solution)/shard_map/all_to_all | solution.py:104
  (97 shorter events, 50.1 us)
Async XLA Ops:
  0.0 95.5 %copy-start = (s32[4,4]{1,0:T(4,128)S(1)}, s32[4,4]{1,0:T(4,128)}, u32[]{:S(2)}) copy-start(s32[4,4]{1,0:T(4,128)} %param.12) | copy-start | bytes 196
  0.0 9.5 %copy-start.1 = (bf16[1,4,48,1536]{3,2,1,0:T(8,128)(2,1)S(1)}, bf16[1,4,48,1536]{3,2,1,0:T(8,128)(2,1)}, u32[]{:S(2)}) copy-start(bf16[1,4,48,1536]{3,2,1,0:T(8,128)(2,1)} %param.10) | copy-start | bytes 1769476
  6.0 12.4 %all-to-all-start.1 = ((bf16[2,2,73728]{2,1,0:T(2,128)(2,1)}), bf16[2,2,73728]{2,1,0:T(2,128)(2,1)S(1)}, u32[]{:S(2)}, u32[]{:S(2)}) async-start(bf16[2,2,73728]{2,1,0:T(2,128)(2,1)} %reshape.67), calls=%async_computation.1 | async-start | bytes 1179648 | tf_op jit(solution)/shard_map/all_to_all | solution.py:67
  18.4 11.6 %all-to-all-start = ((bf16[2,2,73728]{2,1,0:T(2,128)(2,1)}), bf16[2,2,73728]{2,1,0:T(2,128)(2,1)S(1)}, u32[]{:S(2)}, u32[]{:S(2)}) async-start(bf16[2,2,73728]{2,1,0:T(2,128)(2,1)} %reshape.69), calls=%async_computation | async-start | bytes 1179648 | tf_op jit(solution)/shard_map/all_to_all | solution.py:66
  24.9 62.4 %copy-start.2 = (bf16[1,4,48,1536]{3,2,1,0:T(8,128)(2,1)S(1)}, bf16[1,4,48,1536]{3,2,1,0:T(8,128)(2,1)}, u32[]{:S(2)}) copy-start(bf16[1,4,48,1536]{3,2,1,0:T(8,128)(2,1)} %param.9) | copy-start | bytes 1769476
  34.2 51.5 %collective-permute-start = (bf16[1,2,384,768]{3,2,1,0:T(8,128)(2,1)}, bf16[1,2,384,768]{3,2,1,0:T(8,128)(2,1)}, u32[]{:S(2)}, u32[]{:S(2)}) collective-permute-start(bf16[1,2,384,768]{3,2,1,0:T(8,128)(2,1)} %maximum_bitcast_fusion), channel_id=1, source_target_pairs={{0,4},{4,8},{8,12},{12,0},{1,5},{5,9},{9,13},{13,1},{2,6},{6,10},{... | collective-permute-start | bytes 3538952 | tf_op jit(solution)/shard_map/ppermute | solution.py:18
  35.7 75.0 %collective-permute-start.1 = (bf16[1,2,384,768]{3,2,1,0:T(8,128)(2,1)}, bf16[1,2,384,768]{3,2,1,0:T(8,128)(2,1)}, u32[]{:S(2)}, u32[]{:S(2)}) collective-permute-start(bf16[1,2,384,768]{3,2,1,0:T(8,128)(2,1)} %maximum_bitcast_fusion), channel_id=1, source_target_pairs={{0,12},{4,0},{8,4},{12,8},{1,13},{5,1},{9,5},{13,9},{2,14},{6,2},{... | collective-permute-start | bytes 3538952 | tf_op jit(solution)/shard_map/ppermute | solution.py:21
  85.6 29.1 %collective-permute-start.2 = (bf16[1,2,384,768]{3,2,1,0:T(8,128)(2,1)}, bf16[1,2,384,768]{3,2,1,0:T(8,128)(2,1)}, u32[]{:S(2)}, u32[]{:S(2)}) collective-permute-start(bf16[1,2,384,768]{3,2,1,0:T(8,128)(2,1)} %collective-permute-done), channel_id=1, source_target_pairs={{0,4},{4,8},{8,12},{12,0},{1,5},{5,9},{9,13},{13,1},{2,6},{6,10},{... | collective-permute-start | bytes 3538952 | tf_op jit(solution)/shard_map/ppermute | solution.py:18
  91.8 10.4 %all-to-all-start.2 = ((bf16[2,2,73728]{2,1,0:T(2,128)(2,1)}), bf16[2,2,73728]{2,1,0:T(2,128)(2,1)S(1)}, u32[]{:S(2)}, u32[]{:S(2)}) async-start(bf16[2,2,73728]{2,1,0:T(2,128)(2,1)} %reshape.71), calls=%async_computation.2 | async-start | bytes 1179648 | tf_op jit(solution)/shard_map/all_to_all | solution.py:65
  114.7 3.0 %copy-start.3 = (s32[4]{0:T(128)S(1)}, s32[4]{0:T(128)}, u32[]{:S(2)}) copy-start(s32[4]{0:T(128)} %param.13) | copy-start | bytes 52
